TPU v7x, 128 devices: a whole 4x4x4 slice. The times are simulated.
128 devices in a mesh: sec: 4 (over y_hi, core), dev: 32 (over z, y_lo, x).
Axes of the slice: x: 4, y: 4 (y_hi: 2, y_lo: 2; y = y_hi * 2 + y_lo), z: 4, core: 2. Of those that a mesh axis runs over, the one named last changes fastest.
Arguments:
- queries: bfloat16 [256, 8192], P('dev', 'sec')
- fresh_key_value: bfloat16 [2, 256, 512], P(None, 'dev', 'sec'), may hold values from -6 to 6
- key_value_cache: bfloat16 [2, 256, 1024, 512], P(None, 'dev', None, 'sec'), may hold values from -6 to 6
- lengths: int32 [256], P('dev'), may hold values from 1 to 1024, as said below
- residual: bfloat16 [256, 4096], P(None, 'dev'), may hold values from -6 to 6
- out_weight: bfloat16 [8192, 4096], P('sec', 'dev'), may hold values from -0.0625 to 0.0625
- norm_gain: float32 [4096], P('dev'), may hold values from 0.1 to 1.9
- routes: int32 [256, 8], replicated, may hold values from 0 to 63, all different within a row; in each aligned block of 256 rows (0 to 255, 256 to 511, ...) at most 64 rows name the same one
- route_weights: float32 [256, 8], replicated, may hold values from 0.05 to 0.5
- w_gate: bfloat16 [64, 4096, 1536], P('dev', None, 'sec'), may hold values from -0.09375 to 0.09375
- w_up: bfloat16 [64, 4096, 1536], P('dev', None, 'sec'), may hold values from -0.09375 to 0.09375
- w_down: bfloat16 [64, 1536, 4096], P('dev', 'sec'), may hold values from -0.15625 to 0.15625
Outputs:
- layer_out: bfloat16 [256, 4096], P(None, 'dev')
Inputs may be any that keep to these rules, and one draw needn't show every extreme that they name: `routes`: each row names 8 different experts; no expert is named by more than 64 rows, a bound that some block reaches. `lengths`: some row has all 1024 slots filled.
All inputs are finite; a program needn't handle non-finite values.
Results may differ from a plain program's by a relative error of at most 0.0055.
Values may be sent and summed in bfloat16 or wider, within the bound.
No kernel may reach another device: no remote copies, remote signals or barrier semaphores. Data moves between devices by JAX's collectives and lax.ppermute only.
A program may use at most 128 MiB of HBM per device.

v0:
```python
import math
import jax
import jax.numpy as jnp
from jax import lax
from jax.sharding import PartitionSpec as P

D = 4096
QUERY_HEADS = 64
KEY_VALUE_HEADS = 4
HEAD_SIZE = 128
CAP = 64


def attend(queries, fresh_key_value, key_value_cache, lengths):
    row_count = key_value_cache.shape[1]
    cache_length = key_value_cache.shape[2]
    heads_kv = key_value_cache.shape[3] // HEAD_SIZE
    queries_per_group = QUERY_HEADS // KEY_VALUE_HEADS
    score_scale = 1.0 / math.sqrt(HEAD_SIZE)
    head_queries = queries.reshape(row_count, heads_kv, queries_per_group, HEAD_SIZE)
    cached_keys = key_value_cache[0].reshape(row_count, cache_length, heads_kv, HEAD_SIZE)
    cached_values = key_value_cache[1].reshape(row_count, cache_length, heads_kv, HEAD_SIZE)
    own_key = fresh_key_value[0].reshape(row_count, heads_kv, HEAD_SIZE)
    own_value = fresh_key_value[1].reshape(row_count, heads_kv, HEAD_SIZE).astype(jnp.float32)
    scores = (
        jnp.einsum("rkgd,rtkd->rkgt", head_queries, cached_keys, preferred_element_type=jnp.float32)
        * score_scale
    )
    own_score = (
        jnp.einsum("rkgd,rkd->rkg", head_queries, own_key, preferred_element_type=jnp.float32)
        * score_scale
    )
    visible = (jnp.arange(cache_length, dtype=jnp.int32)[None, :] < lengths[:, None])[
        :, None, None, :
    ]
    row_max = jnp.maximum(jnp.max(jnp.where(visible, scores, -jnp.inf), axis=-1), own_score)
    weights = jnp.where(visible, jnp.exp(scores - row_max[..., None]), 0.0)
    own_weight = jnp.exp(own_score - row_max)
    normalizer = jnp.sum(weights, axis=-1) + own_weight
    weighted = jnp.einsum(
        "rkgt,rtkd->rkgd",
        weights.astype(jnp.bfloat16),
        cached_values,
        preferred_element_type=jnp.float32,
    )
    weighted = weighted + own_weight[..., None] * own_value[:, :, None, :]
    return (
        (weighted / normalizer[..., None])
        .astype(jnp.bfloat16)
        .reshape(row_count, heads_kv * queries_per_group * HEAD_SIZE)
    )


def slot_layout(routes, route_weights, expert_ids):
    matches = routes[:, :, None] == expert_ids[None, None, :]
    chosen = jnp.any(matches, axis=1)
    shares = jnp.sum(jnp.where(matches, route_weights[:, :, None], 0.0), axis=1)
    slot_rank = jnp.cumsum(chosen.astype(jnp.int32), axis=0, dtype=jnp.int32) - 1
    slot_ids = jnp.arange(CAP, dtype=jnp.int32)
    slot_mask = (chosen[:, :, None] & (slot_rank[:, :, None] == slot_ids[None, None, :])).transpose(
        1, 2, 0
    )
    spread = slot_mask.astype(jnp.float32) * shares.T[:, None, :]
    return (slot_mask, spread)


def expert_results(full_rows, slot_mask, w_gate, w_up, w_down):
    picked = jnp.einsum(
        "ecr,rd->ecd", slot_mask.astype(jnp.bfloat16), full_rows, preferred_element_type=jnp.float32
    ).astype(jnp.bfloat16)
    gate_part = jnp.einsum("ecd,edf->ecf", picked, w_gate, preferred_element_type=jnp.float32)
    upward = jnp.einsum("ecd,edf->ecf", picked, w_up, preferred_element_type=jnp.float32)
    activation = (jax.nn.silu(gate_part) * upward).astype(jnp.bfloat16)
    return jnp.einsum("ecf,efd->ecd", activation, w_down, preferred_element_type=jnp.float32)


def shards(
    queries,
    fresh_key_value,
    key_value_cache,
    lengths,
    residual,
    out_weight,
    norm_gain,
    routes,
    route_weights,
    w_gate,
    w_up,
    w_down,
):
    attn = attend(queries, fresh_key_value, key_value_cache, lengths)
    partial_out = jnp.dot(
        lax.all_gather(attn, "dev", axis=0, tiled=True),
        out_weight,
        preferred_element_type=jnp.float32,
    )
    hidden = residual.astype(jnp.float32) + lax.psum(partial_out, "sec")
    square_sum = lax.psum(jnp.sum(hidden * hidden, axis=-1, keepdims=True), "dev")
    normed = (hidden * lax.rsqrt(square_sum / D + 1e-06) * norm_gain).astype(jnp.bfloat16)
    full_rows = lax.all_gather(normed, "dev", axis=1, tiled=True)
    local_count = w_gate.shape[0]
    local_ids = lax.axis_index("dev") * local_count + jnp.arange(local_count, dtype=jnp.int32)
    slot_mask, spread = slot_layout(routes, route_weights, local_ids)
    result = expert_results(full_rows, slot_mask, w_gate, w_up, w_down)
    expert_term = jnp.einsum("ecr,ecd->rd", spread, result, precision=lax.Precision.HIGHEST)
    mixture = lax.psum(lax.psum_scatter(expert_term, "dev", scatter_dimension=1, tiled=True), "sec")
    return (hidden + mixture).astype(jnp.bfloat16)


def solution(mesh):
    return jax.shard_map(
        shards,
        mesh=mesh,
        in_specs=(
            P("dev", "sec"),
            P(None, "dev", "sec"),
            P(None, "dev", None, "sec"),
            P("dev"),
            P(None, "dev"),
            P("sec", "dev"),
            P("dev"),
            P(),
            P(),
            P("dev", None, "sec"),
            P("dev", None, "sec"),
            P("dev", "sec", None),
        ),
        out_specs=P(None, "dev"),
        check_vma=False,
    )
```

profile of v0, /device:TPU:1, one launch (start us, length us, event | category | flops | bytes accessed | tf_op | source)
XLA Modules:
  0.0 653.0 jit_solution(15178874167412993256)
XLA Ops:
  6.5 0.0 copy-start
  6.5 0.0 copy-start.2
  6.5 0.0 all-gather.3.cloned.1.call-start
  6.5 0.8 bitcast_convert_fusion
  7.3 0.7 iota_compare_fusion.1
  8.0 0.9 fusion.46
  8.9 0.0 copy-start.5
  8.9 0.0 copy-start.3
  8.9 0.0 copy-start.4
  8.9 2.4 select_reduce_fusion
  11.3 0.2 fusion.24
  11.6 2.1 fusion.21
  13.7 0.6 copy.34
  14.3 0.0 all-gather.3.cloned.1.call-update
  14.3 0.0 all-reduce.3.cloned.1.call-start
  14.4 132.9 %all-gather.3.cloned.1.call-done = bf16[256,2048]{1,0:T(8,128)(2,1)} async-done(((bf16[8,2048]{1,0:T(8,128)(2,1)}), bf16[256,2048]{1,0:T(8,128)(2,1)}) %all-gather.3.cloned.1.call-update) | async-done | bytes 1048592 | tf_op jit(solution)/shard_map/all_gather | solution.py:93
  147.2 0.0 copy-done
  147.2 2.3 fusion.55
  149.5 0.0 all-reduce.3.cloned.1.call-update
  149.5 0.0 all-gather.5.cloned.1.call-start
  149.6 62.2 %all-reduce.3.cloned.1.call-done = f32[256,128]{1,0:T(8,128)} async-done(((f32[256,128]{1,0:T(8,128)}), f32[256,128]{1,0:T(8,128)}) %all-reduce.3.cloned.1.call-update) | async-done | bytes 131088 | tf_op jit(solution)/shard_map/psum | solution.py:97
  211.8 0.0 copy-done.2
  211.8 1.0 multiply_reduce_fusion
  212.9 68.0 %psum.22 = f32[256,1]{0,1:T(1,128)S(1)} all-reduce(f32[256,1]{0,1:T(1,128)S(1)} %bitcast.67), channel_id=1, replica_groups=mesh['sec'=4,'dev'=32] {'dev'}, use_global_device_ids=true, to_apply=%region_8.9 | all-reduce | flops 256 | bytes 2048 | tf_op jit(solution)/shard_map/psum | solution.py:98
  280.9 0.0 copy-done.5
  280.9 1.6 multiply_convert_fusion
  282.5 0.0 all-gather.5.cloned.1.call-update
  282.6 0.0 reduce-scatter.2.cloned.1.call-start
  282.6 0.0 copy-done.3
  282.6 0.1 compare_reduce_fusion
  282.7 0.6 reduce-window.6
  283.4 0.2 slice_reduce_fusion
  283.6 0.2 reduce-window.9
  283.7 0.1 add_bitcast_fusion
  283.8 0.0 copy-done.4
  283.8 0.1 fusion.49
  283.9 116.7 %all-gather.5.cloned.1.call-done = bf16[256,4096]{1,0:T(8,128)(2,1)} async-done(((bf16[256,128]{1,0:T(8,128)(2,1)}), bf16[256,4096]{1,0:T(8,128)(2,1)}) %all-gather.5.cloned.1.call-update) | async-done | bytes 2097168 | tf_op jit(solution)/shard_map/all_gather | solution.py:100
  400.6 2.0 convolution_convert_fusion
  402.6 3.8 fusion.56
  406.4 8.1 %fusion.11 = f32[2,64,4096]{2,1,0:T(8,128)} fusion(bf16[2,384,4096]{2,1,0:T(8,128)(2,1)} %param.23, bf16[2,64,4096]{2,1,0:T(8,128)(2,1)S(1)} %convolution_convert_fusion, bf16[2,4096,384]{2,1,0:T(8,128)(2,1)} %param.22, f32[2,64,384]{2,1,0:T(8,128)S(1)} %fusion.56), kind=kOutput, calls=%fused_computation.12 | convolution fusion | flops 805601280 | bytes 15925248 | tf_op jit(solution)/shard_map/ecf,efd->ecd/dot_general | solution.py:74
  414.5 0.0 copy-start.1
  414.5 6.8 %convolution_bitcast_fusion = f32[256,4096]{1,0:T(8,128)} fusion(f32[2,64,4096]{2,1,0:T(8,128)} %fusion.11, f32[2,256]{1,0:T(2,128)S(1)} %bitcast.65, s32[2,256]{1,0:T(2,128)S(1)} %bitcast.58, pred[2,256]{1,0:T(4,128)(4,1)S(1)} %bitcast.62), kind=kOutput, calls=%fused_computation | convolution fusion | flops 1610711040 | bytes 6296064 | tf_op jit(solution)/shard_map/ecr,ecd->rd/dot_general | solution.py:105
  421.3 0.0 reduce-scatter.2.cloned.1.call-update
  421.3 0.0 all-reduce.5.cloned.1.call-start
  421.4 162.3 %reduce-scatter.2.cloned.1.call-done = f32[256,128]{1,0:T(8,128)} async-done(((f32[256,4096]{1,0:T(8,128)}), f32[256,128]{1,0:T(8,128)}) %reduce-scatter.2.cloned.1.call-update) | async-done | bytes 131088 | tf_op jit(solution)/shard_map/reduce_scatter | solution.py:106
  583.7 0.0 all-reduce.5.cloned.1.call-update
  583.7 61.2 %all-reduce.5.cloned.1.call-done = f32[256,128]{1,0:T(8,128)} async-done(((f32[256,128]{1,0:T(8,128)}), f32[256,128]{1,0:T(8,128)}) %all-reduce.5.cloned.1.call-update) | async-done | bytes 131088 | tf_op jit(solution)/shard_map/psum | solution.py:106
  645.0 0.0 copy-done.1
  645.0 1.6 add_convert_fusion
  (7 shorter events, 0.1 us)
Async XLA Ops:
  6.5 140.7 %copy-start = (bf16[2048,128]{1,0:T(8,128)(2,1)S(1)}, bf16[2048,128]{1,0:T(8,128)(2,1)}, u32[]{:S(2)}) copy-start(bf16[2048,128]{1,0:T(8,128)(2,1)} %param.17) | copy-start | bytes 1572868
  6.5 205.3 %copy-start.2 = (bf16[256,128]{1,0:T(8,128)(2,1)S(1)}, bf16[256,128]{1,0:T(8,128)(2,1)}, u32[]{:S(2)}) copy-start(bf16[256,128]{1,0:T(8,128)(2,1)} %param.16) | copy-start | bytes 196612
  6.5 140.7 %all-gather.3.cloned.1.call-start = ((), (), s32[]{:S(2)}) async-start(), calls=%async_computation.1 | async-start | bytes 1081344 | tf_op jit(solution)/shard_map/all_gather | solution.py:93
  8.9 272.0 %copy-start.5 = (f32[128]{0:T(128)S(1)}, f32[128]{0:T(128)}, u32[]{:S(2)}) copy-start(f32[128]{0:T(128)} %param.18) | copy-start | bytes 1540
  8.9 273.7 %copy-start.3 = (s32[256,8]{0,1:T(8,128)S(1)}, s32[256,8]{0,1:T(8,128)}, u32[]{:S(2)}) copy-start(s32[256,8]{0,1:T(8,128)} %param.19) | copy-start | bytes 24580
  8.9 274.9 %copy-start.4 = (f32[256,8]{0,1:T(8,128)S(1)}, f32[256,8]{0,1:T(8,128)}, u32[]{:S(2)}) copy-start(f32[256,8]{0,1:T(8,128)} %param.20) | copy-start | bytes 24580
  14.3 197.5 %all-reduce.3.cloned.1.call-start = ((), (), s32[]{:S(2)}) async-start(), calls=%async_computation.2 | async-start | bytes 262144 | tf_op jit(solution)/shard_map/psum | solution.py:97
  149.5 251.0 %all-gather.5.cloned.1.call-start = ((), (), s32[]{:S(2)}) async-start(), calls=%async_computation.3 | async-start | bytes 2162688 | tf_op jit(solution)/shard_map/all_gather | solution.py:100
  282.6 301.2 %reduce-scatter.2.cloned.1.call-start = ((), (), s32[]{:S(2)}) async-start(), calls=%async_computation.4 | async-start | bytes 4325376 | tf_op jit(solution)/shard_map/reduce_scatter | solution.py:106
  414.5 230.4 %copy-start.1 = (f32[256,128]{1,0:T(8,128)S(1)}, f32[256,128]{1,0:T(8,128)}, u32[]{:S(2)}) copy-start(f32[256,128]{1,0:T(8,128)} %all-reduce.3.cloned.1.call-done) | copy-start | bytes 393220
  421.3 223.6 %all-reduce.5.cloned.1.call-start = ((), (), s32[]{:S(2)}) async-start(), calls=%async_computation.5 | async-start | bytes 262144 | tf_op jit(solution)/shard_map/psum | solution.py:106
Sparse Core Ops, SparseCore 0:
  14.4 132.7 all-gather.2
  149.7 62.0 all-reduce.2
  282.7 117.8 all-gather.4
  421.4 162.2 reduce-scatter.1
  586.2 58.7 all-reduce.4
where the time goes:
time: 654 us; the launch traced here: 653 us
  waiting for transfers between devices  535 us (82%)
  blocking collectives  68 us (10%)
  matrix products  28.3 us (4%)
  between operations  13.2 us (2%)
  other arithmetic  7.04 us (1%)
    reduce_scatter x1, waiting for transfers between devices, shards(): lax.psum_scatter(expert_term, 'dev', scatter_dimension=1, tiled=True)  162 us
    all_gather x1, waiting for transfers between devices, shards(): lax.all_gather(attn, 'dev', axis=0, tiled=True)  133 us
    all_gather x1, waiting for transfers between devices, shards(): full_rows = lax.all_gather(normed, 'dev', axis=1, tiled=True)  117 us
    psum x1, blocking collectives, shards(): lax.psum(jnp.sum(hidden * hidden, axis=-1, keepdims=True), 'dev')  68 us
    psum x1, waiting for transfers between devices, shards(): hidden = residual.astype(jnp.float32) + lax.psum(partial_out, 'sec')  62.2 us
    psum x1, waiting for transfers between devices, shards(): lax.psum(lax.psum_scatter(expert_term, 'dev', scatter_dimension=1, tiled=...  61.2 us
  transfers between devices with their start and end apart: 5, of which 5 were waited for; matrix products, arithmetic and copies ran while one was open for 0% of the time, Pallas kernels for 0%

commit v1 on v0

--- a/solution.py
+++ b/solution.py
@@ -103,7 +103,12 @@
     slot_mask, spread = slot_layout(routes, route_weights, local_ids)
     result = expert_results(full_rows, slot_mask, w_gate, w_up, w_down)
     expert_term = jnp.einsum("ecr,ecd->rd", spread, result, precision=lax.Precision.HIGHEST)
-    mixture = lax.psum(lax.psum_scatter(expert_term, "dev", scatter_dimension=1, tiled=True), "sec")
+    mixture = jnp.sum(
+        lax.all_gather(
+            lax.psum_scatter(expert_term, "dev", scatter_dimension=1, tiled=True), "sec"
+        ),
+        axis=0,
+    )
     return (hidden + mixture).astype(jnp.bfloat16)
 
 

time: 654 us -> 623 us (0.953)
  waiting for transfers between devices: 535 us -> 474 us
  blocking collectives: 68 us -> 99.4 us
    psum x1 -> x0, waiting for transfers between devices: 61.2 us -> none  [shards(): lax.psum(lax.psum_scatter(expert_term, 'dev', scatter_dimension=1, tiled=...]
    all_gather x0 -> x1, blocking collectives: none -> 31.4 us  [shards(): lax.all_gather(lax.psum_scatter(expert_term, 'dev', scatter_dimension=1,...]
  transfers between devices with their start and end apart: 5 -> 4, of which waited for: 5 -> 4; matrix products, arithmetic and copies ran while one was open for 0% -> 0% of each run, Pallas kernels for 0% -> 0%
where the time goes in v1:
time: 623 us; the launch traced here: 622 us
  waiting for transfers between devices  474 us (76%)
  blocking collectives  99.4 us (16%)
  matrix products  28.3 us (5%)
  between operations  13.2 us (2%)
    reduce_scatter x1, waiting for transfers between devices, shards(): lax.psum_scatter(expert_term, 'dev', scatter_dimension=1, tiled=True)  162 us
    all_gather x1, waiting for transfers between devices, shards(): lax.all_gather(attn, 'dev', axis=0, tiled=True)  133 us
    all_gather x1, waiting for transfers between devices, shards(): full_rows = lax.all_gather(normed, 'dev', axis=1, tiled=True)  117 us
    psum x1, blocking collectives, shards(): lax.psum(jnp.sum(hidden * hidden, axis=-1, keepdims=True), 'dev')  68 us
    psum x1, waiting for transfers between devices, shards(): hidden = residual.astype(jnp.float32) + lax.psum(partial_out, 'sec')  62.2 us
    all_gather x1, blocking collectives, shards(): lax.all_gather(lax.psum_scatter(expert_term, 'dev', scatter_dimension=1,...  31.4 us
  transfers between devices with their start and end apart: 4, of which 4 were waited for; matrix products, arithmetic and copies ran while one was open for 0% of the time, Pallas kernels for 0%

profile of v1, /device:TPU:1, one launch (start us, length us, event | category | flops | bytes accessed | tf_op | source)
XLA Modules:
  0.0 622.3 jit_solution(15297765289965824629)
XLA Ops:
  6.5 0.0 copy-start
  6.5 0.0 copy-start.2
  6.5 0.0 all-gather.4.cloned.1.call-start
  6.5 0.8 bitcast_convert_fusion
  7.3 0.7 iota_compare_fusion.1
  8.0 0.9 fusion.46
  8.9 0.0 copy-start.5
  8.9 0.0 copy-start.3
  8.9 0.0 copy-start.4
  8.9 2.4 select_reduce_fusion
  11.3 0.2 fusion.24
  11.6 2.1 fusion.21
  13.7 0.6 copy.34
  14.3 0.0 all-gather.4.cloned.1.call-update
  14.3 0.0 all-reduce.2.cloned.1.call-start
  14.4 132.9 %all-gather.4.cloned.1.call-done = bf16[256,2048]{1,0:T(8,128)(2,1)} async-done(((bf16[8,2048]{1,0:T(8,128)(2,1)}), bf16[256,2048]{1,0:T(8,128)(2,1)}) %all-gather.4.cloned.1.call-update) | async-done | bytes 1048592 | tf_op jit(solution)/shard_map/all_gather | solution.py:93
  147.2 0.0 copy-done
  147.2 2.3 fusion.55
  149.5 0.0 all-reduce.2.cloned.1.call-update
  149.5 0.0 all-gather.6.cloned.1.call-start
  149.6 62.2 %all-reduce.2.cloned.1.call-done = f32[256,128]{1,0:T(8,128)} async-done(((f32[256,128]{1,0:T(8,128)}), f32[256,128]{1,0:T(8,128)}) %all-reduce.2.cloned.1.call-update) | async-done | bytes 131088 | tf_op jit(solution)/shard_map/psum | solution.py:97
  211.8 0.0 copy-done.2
  211.8 1.0 multiply_reduce_fusion
  212.9 68.0 %psum.15 = f32[256,1]{0,1:T(1,128)S(1)} all-reduce(f32[256,1]{0,1:T(1,128)S(1)} %bitcast.69), channel_id=1, replica_groups=mesh['sec'=4,'dev'=32] {'dev'}, use_global_device_ids=true, to_apply=%region_8.9 | all-reduce | flops 256 | bytes 2048 | tf_op jit(solution)/shard_map/psum | solution.py:98
  280.9 0.0 copy-done.5
  280.9 1.6 multiply_convert_fusion
  282.5 0.0 all-gather.6.cloned.1.call-update
  282.6 0.0 reduce-scatter.2.cloned.1.call-start
  282.6 0.0 copy-done.3
  282.6 0.1 compare_reduce_fusion
  282.7 0.6 reduce-window.6
  283.4 0.2 slice_reduce_fusion
  283.6 0.2 reduce-window.9
  283.7 0.1 add_bitcast_fusion
  283.8 0.0 copy-done.4
  283.8 0.1 fusion.49
  283.9 116.7 %all-gather.6.cloned.1.call-done = bf16[256,4096]{1,0:T(8,128)(2,1)} async-done(((bf16[256,128]{1,0:T(8,128)(2,1)}), bf16[256,4096]{1,0:T(8,128)(2,1)}) %all-gather.6.cloned.1.call-update) | async-done | bytes 2097168 | tf_op jit(solution)/shard_map/all_gather | solution.py:100
  400.6 2.0 convolution_convert_fusion
  402.6 3.8 fusion.56
  406.4 8.1 %fusion.11 = f32[2,64,4096]{2,1,0:T(8,128)} fusion(bf16[2,384,4096]{2,1,0:T(8,128)(2,1)} %param.23, bf16[2,64,4096]{2,1,0:T(8,128)(2,1)S(1)} %convolution_convert_fusion, bf16[2,4096,384]{2,1,0:T(8,128)(2,1)} %param.22, f32[2,64,384]{2,1,0:T(8,128)S(1)} %fusion.56), kind=kOutput, calls=%fused_computation.12 | convolution fusion | flops 805601280 | bytes 15925248 | tf_op jit(solution)/shard_map/ecf,efd->ecd/dot_general | solution.py:74
  414.5 6.7 %convolution_bitcast_fusion = f32[256,4096]{1,0:T(8,128)} fusion(f32[2,64,4096]{2,1,0:T(8,128)} %fusion.11, f32[2,256]{1,0:T(2,128)S(1)} %bitcast.67, s32[2,256]{1,0:T(2,128)S(1)} %bitcast.60, pred[2,256]{1,0:T(4,128)(4,1)S(1)} %bitcast.64), kind=kOutput, calls=%fused_computation | convolution fusion | flops 1610711040 | bytes 6296064 | tf_op jit(solution)/shard_map/ecr,ecd->rd/dot_general | solution.py:105
  421.2 0.0 copy-start.1
  421.2 0.0 reduce-scatter.2.cloned.1.call-update
  421.3 162.4 %reduce-scatter.2.cloned.1.call-done = f32[256,128]{1,0:T(8,128)} async-done(((f32[256,4096]{1,0:T(8,128)}), f32[256,128]{1,0:T(8,128)}) %reduce-scatter.2.cloned.1.call-update) | async-done | bytes 131088 | tf_op jit(solution)/shard_map/reduce_scatter | solution.py:108
  583.6 31.4 %all-gather = f32[1024,128]{1,0:T(8,128)S(1)} all-gather(f32[256,128]{1,0:T(8,128)} %reduce-scatter.2.cloned.1.call-done), channel_id=2, replica_groups=mesh['sec'=4,'dev'=32] {'sec'}, dimensions={0}, use_global_device_ids=true | all-gather | bytes 655360 | tf_op jit(solution)/shard_map/all_gather | solution.py:107
  615.1 0.0 copy-done.1
  615.1 0.7 add_convert_fusion
  (8 shorter events, 0.1 us)
Async XLA Ops:
  6.5 140.7 %copy-start = (bf16[2048,128]{1,0:T(8,128)(2,1)S(1)}, bf16[2048,128]{1,0:T(8,128)(2,1)}, u32[]{:S(2)}) copy-start(bf16[2048,128]{1,0:T(8,128)(2,1)} %param.17) | copy-start | bytes 1572868
  6.5 205.3 %copy-start.2 = (bf16[256,128]{1,0:T(8,128)(2,1)S(1)}, bf16[256,128]{1,0:T(8,128)(2,1)}, u32[]{:S(2)}) copy-start(bf16[256,128]{1,0:T(8,128)(2,1)} %param.16) | copy-start | bytes 196612
  6.5 140.7 %all-gather.4.cloned.1.call-start = ((), (), s32[]{:S(2)}) async-start(), calls=%async_computation.1 | async-start | bytes 1081344 | tf_op jit(solution)/shard_map/all_gather | solution.py:93
  8.9 272.0 %copy-start.5 = (f32[128]{0:T(128)S(1)}, f32[128]{0:T(128)}, u32[]{:S(2)}) copy-start(f32[128]{0:T(128)} %param.18) | copy-start | bytes 1540
  8.9 273.7 %copy-start.3 = (s32[256,8]{0,1:T(8,128)S(1)}, s32[256,8]{0,1:T(8,128)}, u32[]{:S(2)}) copy-start(s32[256,8]{0,1:T(8,128)} %param.19) | copy-start | bytes 24580
  8.9 274.9 %copy-start.4 = (f32[256,8]{0,1:T(8,128)S(1)}, f32[256,8]{0,1:T(8,128)}, u32[]{:S(2)}) copy-start(f32[256,8]{0,1:T(8,128)} %param.20) | copy-start | bytes 24580
  14.3 197.5 %all-reduce.2.cloned.1.call-start = ((), (), s32[]{:S(2)}) async-start(), calls=%async_computation.2 | async-start | bytes 262144 | tf_op jit(solution)/shard_map/psum | solution.py:97
  149.5 251.0 %all-gather.6.cloned.1.call-start = ((), (), s32[]{:S(2)}) async-start(), calls=%async_computation.3 | async-start | bytes 2162688 | tf_op jit(solution)/shard_map/all_gather | solution.py:100
  282.6 301.1 %reduce-scatter.2.cloned.1.call-start = ((), (), s32[]{:S(2)}) async-start(), calls=%async_computation.4 | async-start | bytes 4325376 | tf_op jit(solution)/shard_map/reduce_scatter | solution.py:108
  421.2 193.8 %copy-start.1 = (f32[256,128]{1,0:T(8,128)S(1)}, f32[256,128]{1,0:T(8,128)}, u32[]{:S(2)}) copy-start(f32[256,128]{1,0:T(8,128)} %all-reduce.2.cloned.1.call-done) | copy-start | bytes 393220
Sparse Core Ops, SparseCore 0:
  14.4 132.7 all-gather.3
  149.7 62.0 all-reduce.1
  282.7 117.8 all-gather.5
  421.4 162.2 reduce-scatter.1
